TPU v7x, 32 devices: a whole 2x2x4 slice. The times are simulated.
32 devices in a mesh: dp: 16 (over z, y, x), mp: 2 (over core).
Axes of the slice: x: 2, y: 2, z: 4, core: 2. Of those that a mesh axis runs over, the one named last changes fastest.
Arguments:
- store_rows: bfloat16 [8192, 4096], P('dp', 'mp'), may hold values from -64 to 64
- norm_gain: bfloat16 [4096], replicated, may hold values from 0.099609375 to 1.8984375
- key_weight: bfloat16 [4096, 2048], P(None, 'mp'), may hold values from -0.09375 to 0.09375
- value_weight: bfloat16 [4096, 2048], P(None, 'mp'), may hold values from -0.09375 to 0.09375
- queries: bfloat16 [128, 2048], P('dp', 'mp'), may hold values from -300 to 300
- counts: int32 [16], replicated, may hold values from 1 to 8, 32 in all
- slot_plan: int32 [32], P('dp'), may hold values from 0 to 31, each once
Outputs:
- context: bfloat16 [128, 2048], P('dp', 'mp')
All inputs are finite; a program needn't handle non-finite values.
Results may differ from a plain program's by a relative error of at most 0.0091.
Values may be sent and summed in bfloat16 or wider, within the bound.
A program may use at most 64 MiB of HBM per device.

v0:
```python
import jax
import jax.numpy as jnp
from jax import lax
from jax.sharding import PartitionSpec as P

HEAD_DIM = 64
norm_eps = 1e-06
score_scale = 0.125
far_below = -1e30


def local(store_rows, norm_gain, key_weight, value_weight, queries, counts, slot_plan):
    full_width = norm_gain.shape[0]
    row_count = store_rows.shape[0]
    local_cols = store_rows.shape[1]
    head_cols = key_weight.shape[1]
    heads_here = head_cols // HEAD_DIM
    passages_here = slot_plan.shape[0]
    seq_len = row_count // passages_here
    gain_full = norm_gain.astype(jnp.float32)
    raw_rows = store_rows.astype(jnp.float32)
    own_gain = lax.dynamic_slice_in_dim(gain_full, lax.axis_index("mp") * local_cols, local_cols, 0)
    scaled = (raw_rows * own_gain[None, :]).astype(jnp.bfloat16)
    total_sq = lax.psum(jnp.sum(raw_rows * raw_rows, axis=1), "mp")
    shard_part = lax.all_gather(scaled, "mp", axis=1, tiled=True)
    key_acc = jnp.dot(shard_part, key_weight, preferred_element_type=jnp.float32)
    value_acc = jnp.dot(shard_part, value_weight, preferred_element_type=jnp.float32)
    inv_rms = lax.rsqrt(total_sq / full_width + norm_eps)
    key_rows = (key_acc * inv_rms[:, None]).astype(jnp.bfloat16)
    value_rows = (value_acc * inv_rms[:, None]).astype(jnp.bfloat16)
    ends = jnp.cumsum(counts)
    slot_question = jnp.sum((slot_plan[:, None] >= ends[None, :]).astype(jnp.int32), axis=1)
    num_questions = counts.shape[0]
    dec_len = queries.shape[0]
    gathered = lax.all_gather(queries, "dp", axis=0, tiled=True)
    query_table = gathered.reshape(num_questions, dec_len, heads_here, HEAD_DIM)
    slot_queries = jnp.take(query_table, slot_question, axis=0)
    key_blocks = key_rows.reshape(passages_here, seq_len, heads_here, HEAD_DIM)
    value_blocks = value_rows.reshape(passages_here, seq_len, heads_here, HEAD_DIM).astype(
        jnp.float32
    )
    scores = (
        jnp.einsum("pihd,pthd->piht", slot_queries, key_blocks, preferred_element_type=jnp.float32)
        * score_scale
    )
    slot_max = jnp.max(scores, axis=3)
    member = slot_question[None, :] == jnp.arange(num_questions, dtype=jnp.int32)[:, None]
    member_float = member.astype(jnp.float32)
    question_max = jnp.max(jnp.where(member[:, :, None, None], slot_max[None], far_below), axis=1)
    max_level = lax.pmax(question_max, "dp")
    slot_level = jnp.take(max_level, slot_question, axis=0)
    weights = jnp.exp(scores - slot_level[..., None])
    slot_den = jnp.sum(weights, axis=3)
    slot_num = jnp.einsum("piht,pthd->pihd", weights, value_blocks, precision=lax.Precision.HIGHEST)
    slot_num = slot_num.reshape(passages_here, dec_len, head_cols)
    numerator = jnp.einsum("qp,pik->qik", member_float, slot_num, precision=lax.Precision.HIGHEST)
    denominator = jnp.einsum("qp,pih->qih", member_float, slot_den, precision=lax.Precision.HIGHEST)
    numerator, denominator = (numerator, denominator)
    summed_num, summed_den = (
        lax.psum_scatter(numerator, "dp", scatter_dimension=0, tiled=True),
        lax.psum_scatter(denominator, "dp", scatter_dimension=0, tiled=True),
    )
    own_num = summed_num[0]
    own_den = summed_den[0]
    context = own_num.reshape(dec_len, heads_here, HEAD_DIM) / own_den[..., None]
    return context.reshape(dec_len, head_cols).astype(jnp.bfloat16)


def solution(mesh):
    placed = (P("dp", "mp"), P(), P(None, "mp"), P(None, "mp"), P("dp", "mp"), P(), P("dp"))
    return jax.shard_map(
        local, mesh=mesh, in_specs=placed, out_specs=P("dp", "mp"), check_vma=False
    )
```

profile of v0, /device:TPU:0, one launch (start us, length us, event | category | flops | bytes accessed | tf_op | source)
XLA Modules:
  0.0 241.7 jit_solution(15678639214267508043)
XLA Ops:
  6.5 0.7 dynamic-slice_convert_fusion
  7.2 3.5 %fusion.1 = (f32[512]{0:T(512)S(1)}, bf16[512,2048]{1,0:T(8,128)(2,1)}) fusion(bf16[512,2048]{1,0:T(8,128)(2,1)} %param.7, f32[2048]{0:T(1024)S(1)} %dynamic-slice_convert_fusion), kind=kLoop, calls=%fused_computation.5 | loop fusion | flops 5242368 | bytes 4204544 | tf_op jit(solution)/shard_map/reduce_sum | solution.py:24
  10.8 0.6 copy-done.1
  11.4 0.1 copy.36
  11.5 0.1 reduce
  11.7 0.2 fusion.23
  11.8 0.1 iota_compare_fusion
  11.9 0.1 copy.41
  12.0 43.8 %all_gather.7 = bf16[128,1024]{1,0:T(8,128)(2,1)S(1)} all-gather(bf16[8,1024]{1,0:T(8,128)(2,1)S(1)} %copy-done), channel_id=1, replica_groups=mesh['dp'=16,'mp'=2] {'dp'}, dimensions={0}, use_global_device_ids=true | all-gather | bytes 278528 | tf_op jit(solution)/shard_map/all_gather | solution.py:35
  55.8 0.3 reshape.86
  56.2 0.6 gather_fusion
  56.7 2.5 %psum.7 = f32[512]{0:T(512)S(1)} all-reduce(f32[512]{0:T(512)S(1)} %get-tuple-element.5), channel_id=1, replica_groups=mesh['dp'=16,'mp'=2] {'mp'}, use_global_device_ids=true, to_apply=%region_3.4 | all-reduce | flops 512 | bytes 4096 | tf_op jit(solution)/shard_map/psum | solution.py:24
  59.2 0.1 broadcast_select_fusion
  59.3 9.1 %multiply_convert_fusion.1 = bf16[512,1024]{1,0:T(8,128)(2,1)S(1)} fusion(bf16[512,4096]{1,0:T(8,128)(2,1)} %all-gather.2.cloned.1.call-done, bf16[4096,1024]{1,0:T(8,128)(2,1)} %param.10, f32[512]{0:T(512)S(1)} %add_rsqrt_fusion), kind=kOutput, calls=%fused_computation.11 | convolution fusion | flops 4296015872 | bytes 13633536 | tf_op jit(solution)/shard_map/dot_general | solution.py:27
  68.4 1.3 reshape.105
  69.8 9.1 %multiply_convert_fusion = bf16[512,1024]{1,0:T(8,128)(2,1)S(1)} fusion(bf16[512,4096]{1,0:T(8,128)(2,1)} %all-gather.2.cloned.1.call-done, bf16[4096,1024]{1,0:T(8,128)(2,1)} %param.9, f32[512]{0:T(512)S(1)} %add_rsqrt_fusion), kind=kOutput, calls=%fused_computation.10 | convolution fusion | flops 4296015872 | bytes 13633536 | tf_op jit(solution)/shard_map/dot_general | solution.py:26
  78.9 2.4 reshape.106
  81.3 2.3 fusion.25
  83.7 0.1 select_reduce_fusion
  83.8 72.0 %pmax.7 = f32[16,8,16]{2,1,0:T(8,128)S(1)} all-reduce(f32[16,8,16]{2,1,0:T(8,128)S(1)} %select_reduce_fusion), channel_id=1, replica_groups=mesh['dp'=16,'mp'=2] {'dp'}, use_global_device_ids=true, to_apply=%region_6.7 | all-reduce | flops 2048 | bytes 16384 | tf_op jit(solution)/shard_map/pmax | solution.py:50
  155.8 0.5 gather_fusion.1
  156.5 1.2 fusion.12
  157.8 0.1 reshape.107
  157.9 0.5 fusion.21
  158.4 1.1 copy.47
  159.5 0.6 dynamic-slice
  160.1 0.2 fusion.15
  160.4 0.3 fusion.19
  160.7 71.9 %all-reduce = f32[16,8,16]{2,1,0:T(8,128)S(1)} all-reduce(f32[16,8,16]{2,1,0:T(8,128)S(1)} %copy.49), channel_id=3, replica_groups=mesh['dp'=16,'mp'=2] {'dp'}, use_global_device_ids=true, to_apply=%region_9.10.clone | all-reduce | flops 2048 | bytes 16384
  232.7 0.6 dynamic-slice_bitcast_fusion
  233.4 0.1 div.23
  233.5 1.4 fusion.18
  (25 shorter events, 0.6 us)
Async XLA Ops:
  6.5 52.8 %all-gather.2.cloned.1.call-start = ((), (), s32[]{:S(2)}) async-start(), calls=%async_computation.1 | async-start | bytes 6291456 | tf_op jit(solution)/shard_map/all_gather | solution.py:25
  10.8 0.7 copy-start.1
  10.8 0.9 copy-start.2
  10.8 1.3 copy-start
  10.8 222.7 %reduce-scatter.2.cloned.1.call-start = ((), (), s32[]{:S(2)}) async-start(), calls=%async_computation.2 | async-start | bytes 557056 | tf_op jit(solution)/shard_map/reduce_scatter | solution.py:60
  157.7 1.8 copy-start.3
Sparse Core Ops, SparseCore 0:
  10.9 16.3 all-gather.1
  159.6 72.4 reduce-scatter.1
where the time goes:
time: 242 us
  blocking collectives  190 us (79%)
  matrix products  22.6 us (9%)
  between operations  13.6 us (6%)
  local copies, waits for them, and re-layouts  8.82 us (4%)
  other arithmetic  6.49 us (3%)
    pmax x1, blocking collectives, local(): max_level = lax.pmax(question_max, 'dp')  72 us
    unnamed x1, blocking collectives  71.9 us
    all_gather x1, blocking collectives, local(): gathered = lax.all_gather(queries, 'dp', axis=0, tiled=True)  43.8 us
    dot_general x1, matrix products, local(): jnp.dot(shard_part, key_weight, preferred_element_type=jnp.float32)  9.15 us
    dot_general x1, matrix products, local(): jnp.dot(shard_part, value_weight, preferred_element_type=jnp.float32)  9.15 us
  transfers between devices with their start and end apart: 2, of which 0 were waited for; matrix products, arithmetic and copies ran while one was open for 1% of the time, Pallas kernels for 0%

commit v1 on v0

--- a/solution.py
+++ b/solution.py
@@ -32,7 +32,14 @@
     slot_question = jnp.sum((slot_plan[:, None] >= ends[None, :]).astype(jnp.int32), axis=1)
     num_questions = counts.shape[0]
     dec_len = queries.shape[0]
-    gathered = lax.all_gather(queries, "dp", axis=0, tiled=True)
+    ways, here, step = (lax.axis_size("dp"), lax.axis_index("dp"), queries.shape[0])
+    line, have = (queries, 1)
+    while have < ways:
+        line = jnp.concatenate(
+            [line, lax.ppermute(line, "dp", [(d, (d - have) % ways) for d in range(ways)])], axis=0
+        )
+        have = 2 * have
+    gathered = jnp.roll(line, here * step, axis=0)
     query_table = gathered.reshape(num_questions, dec_len, heads_here, HEAD_DIM)
     slot_queries = jnp.take(query_table, slot_question, axis=0)
     key_blocks = key_rows.reshape(passages_here, seq_len, heads_here, HEAD_DIM)

time: 242 us -> 228 us (0.942)
  blocking collectives: 190 us -> 154 us
  waiting for transfers between devices: 0.05 us -> 13.7 us
  starting transfers between devices: 0.04 us -> 8.05 us
    all_gather x1 -> x0, blocking collectives: 43.8 us -> none  [local(): gathered = lax.all_gather(queries, 'dp', axis=0, tiled=True)]
    ppermute x0 -> x4, waiting for transfers between devices: none -> 13.7 us  [local(): lax.ppermute(line, 'dp', [(d, (d - have) % ways) for d in range(ways)])]
    ppermute x0 -> x4, starting transfers between devices: none -> 8.01 us  [local(): lax.ppermute(line, 'dp', [(d, (d - have) % ways) for d in range(ways)])]
    pmax x1, blocking collectives: 72 us -> 79.7 us  [local(): max_level = lax.pmax(question_max, 'dp')]
  transfers between devices with their start and end apart: 2 -> 6, of which waited for: 0 -> 3; matrix products, arithmetic and copies ran while one was open for 1% -> 2% of each run, Pallas kernels for 0% -> 0%
where the time goes in v1:
time: 228 us
  blocking collectives  154 us (68%)
  matrix products  22.6 us (10%)
  waiting for transfers between devices  13.7 us (6%)
  between operations  13.6 us (6%)
  local copies, waits for them, and re-layouts  8.97 us (4%)
  starting transfers between devices  8.05 us (4%)
  other arithmetic  6.51 us (3%)
    pmax x1, blocking collectives, local(): max_level = lax.pmax(question_max, 'dp')  79.7 us
    unnamed x1, blocking collectives  72 us
    ppermute x4, waiting for transfers between devices, local(): lax.ppermute(line, 'dp', [(d, (d - have) % ways) for d in range(ways)])  13.7 us
    dot_general x1, matrix products, local(): jnp.dot(shard_part, key_weight, preferred_element_type=jnp.float32)  9.15 us
    dot_general x1, matrix products, local(): jnp.dot(shard_part, value_weight, preferred_element_type=jnp.float32)  9.15 us
    ppermute x4, starting transfers between devices, local(): lax.ppermute(line, 'dp', [(d, (d - have) % ways) for d in range(ways)])  8.01 us
  transfers between devices with their start and end apart: 6, of which 3 were waited for; matrix products, arithmetic and copies ran while one was open for 2% of the time, Pallas kernels for 0%

profile of v1, /device:TPU:0, one launch (start us, length us, event | category | flops | bytes accessed | tf_op | source)
XLA Modules:
  0.0 227.7 jit_solution(8624072191167993610)
XLA Ops:
  6.5 0.7 dynamic-slice_convert_fusion
  7.2 3.5 %fusion.1 = (f32[512]{0:T(512)S(1)}, bf16[512,2048]{1,0:T(8,128)(2,1)}) fusion(bf16[512,2048]{1,0:T(8,128)(2,1)} %param.7, f32[2048]{0:T(1024)S(1)} %dynamic-slice_convert_fusion), kind=kLoop, calls=%fused_computation.5 | loop fusion | flops 5242368 | bytes 4204544 | tf_op jit(solution)/shard_map/reduce_sum | solution.py:24
  10.8 0.6 copy-done
  11.5 6.9 %collective-permute-start = (bf16[8,1024]{1,0:T(8,128)(2,1)S(1)}, bf16[8,1024]{1,0:T(8,128)(2,1)S(1)}, u32[]{:S(2)}, u32[]{:S(2)}) collective-permute-start(bf16[8,1024]{1,0:T(8,128)(2,1)S(1)} %copy-done), channel_id=1, source_target_pairs={{0,30},{2,0},{4,2},{6,4},{8,6},{10,8},{12,10},{14,12},{16,14},{18,... | collective-permute-start | bytes 49160 | tf_op jit(solution)/shard_map/ppermute | solution.py:39
  18.5 0.1 reduce
  18.7 2.5 %psum.7 = f32[512]{0:T(512)S(1)} all-reduce(f32[512]{0:T(512)S(1)} %get-tuple-element.5), channel_id=1, replica_groups=mesh['dp'=16,'mp'=2] {'mp'}, use_global_device_ids=true, to_apply=%region_3.4 | all-reduce | flops 512 | bytes 4096 | tf_op jit(solution)/shard_map/psum | solution.py:24
  21.1 0.2 fusion.23
  21.4 0.6 collective-permute-start.1
  22.1 3.3 %collective-permute-done.1 = bf16[16,1024]{1,0:T(8,128)(2,1)S(1)} collective-permute-done((bf16[16,1024]{1,0:T(8,128)(2,1)S(1)}, bf16[16,1024]{1,0:T(8,128)(2,1)S(1)}, u32[]{:S(2)}, u32[]{:S(2)}) %collective-permute-start.1) | collective-permute-done | bytes 32800 | tf_op jit(solution)/shard_map/ppermute | solution.py:39
  25.4 0.4 collective-permute-start.2
  25.8 3.8 %collective-permute-done.2 = bf16[32,1024]{1,0:T(8,128)(2,1)S(1)} collective-permute-done((bf16[32,1024]{1,0:T(8,128)(2,1)S(1)}, bf16[32,1024]{1,0:T(8,128)(2,1)S(1)}, u32[]{:S(2)}, u32[]{:S(2)}) %collective-permute-start.2) | collective-permute-done | bytes 65568 | tf_op jit(solution)/shard_map/ppermute | solution.py:39
  29.8 6.6 %collective-permute-done.3 = bf16[64,1024]{1,0:T(8,128)(2,1)S(1)} collective-permute-done((bf16[64,1024]{1,0:T(8,128)(2,1)S(1)}, bf16[64,1024]{1,0:T(8,128)(2,1)S(1)}, u32[]{:S(2)}, u32[]{:S(2)}) %collective-permute-start.3) | collective-permute-done | bytes 131104 | tf_op jit(solution)/shard_map/ppermute | solution.py:39
  36.5 0.3 reshape.86
  36.8 0.6 gather_fusion
  37.5 9.1 %multiply_convert_fusion.1 = bf16[512,1024]{1,0:T(8,128)(2,1)S(1)} fusion(bf16[512,4096]{1,0:T(8,128)(2,1)} %all-gather.2.cloned.1.call-done, bf16[4096,1024]{1,0:T(8,128)(2,1)} %param.10, f32[512]{0:T(512)S(1)} %add_rsqrt_fusion), kind=kOutput, calls=%fused_computation.11 | convolution fusion | flops 4296015872 | bytes 13633536 | tf_op jit(solution)/shard_map/dot_general | solution.py:27
  46.6 1.3 reshape.105
  48.0 9.1 %multiply_convert_fusion = bf16[512,1024]{1,0:T(8,128)(2,1)S(1)} fusion(bf16[512,4096]{1,0:T(8,128)(2,1)} %all-gather.2.cloned.1.call-done, bf16[4096,1024]{1,0:T(8,128)(2,1)} %param.9, f32[512]{0:T(512)S(1)} %add_rsqrt_fusion), kind=kOutput, calls=%fused_computation.10 | convolution fusion | flops 4296015872 | bytes 13633536 | tf_op jit(solution)/shard_map/dot_general | solution.py:26
  57.1 2.4 %reshape.106 = bf16[2,256,16,64]{3,2,1,0:T(8,128)(2,1)} reshape(bf16[512,1024]{1,0:T(8,128)(2,1)S(1)} %multiply_convert_fusion) | data formatting | bytes 2097152 | tf_op jit(solution)/shard_map/reshape | solution.py:45
  59.5 2.3 %fusion.25 = (f32[2,8,16]{1,2,0:T(8,128)S(1)}, f32[2,8,16,256]{3,1,2,0:T(8,128)S(1)}) fusion(bf16[2,8,16,64]{3,2,1,0:T(8,128)(2,1)S(1)} %broadcast_select_fusion, bf16[2,256,16,64]{3,2,1,0:T(8,128)(2,1)} %reshape.106), kind=kOutput, calls=%fused_computation.53 | convolution fusion | flops 8519424 | bytes 1344512 | tf_op jit(solution)/shard_map/pihd,pthd->piht/dot_general | solution.py:50
  61.9 0.1 select_reduce_fusion
  62.0 79.7 %pmax.7 = f32[16,8,16]{2,1,0:T(8,128)S(1)} all-reduce(f32[16,8,16]{2,1,0:T(8,128)S(1)} %select_reduce_fusion), channel_id=1, replica_groups=mesh['dp'=16,'mp'=2] {'dp'}, use_global_device_ids=true, to_apply=%region_6.7 | all-reduce | flops 2048 | bytes 16384 | tf_op jit(solution)/shard_map/pmax | solution.py:57
  141.7 0.5 gather_fusion.1
  142.5 1.2 fusion.12
  143.7 0.1 reshape.107
  143.8 0.5 fusion.21
  144.3 1.1 copy.47
  145.5 0.6 dynamic-slice
  146.1 0.2 fusion.15
  146.3 0.3 fusion.19
  146.7 72.0 %all-reduce = f32[16,8,16]{2,1,0:T(8,128)S(1)} all-reduce(f32[16,8,16]{2,1,0:T(8,128)S(1)} %copy.49), channel_id=3, replica_groups=mesh['dp'=16,'mp'=2] {'dp'}, use_global_device_ids=true, to_apply=%region_9.10.clone | all-reduce | flops 2048 | bytes 16384
  218.7 0.6 dynamic-slice_bitcast_fusion
  219.5 1.4 fusion.18
  (46 shorter events, 1.2 us)
Async XLA Ops:
  6.5 30.9 %all-gather.2.cloned.1.call-start = ((), (), s32[]{:S(2)}) async-start(), calls=%async_computation.1 | async-start | bytes 6291456 | tf_op jit(solution)/shard_map/all_gather | solution.py:25
  10.8 0.7 copy-start
  10.8 7.7 %copy-start.1 = (s32[16]{0:T(128)S(1)}, s32[16]{0:T(128)}, u32[]{:S(2)}) copy-start(s32[16]{0:T(128)} %param.12) | copy-start | bytes 196
  10.8 10.4 %copy-start.2 = (s32[2]{0:T(128)S(1)}, s32[2]{0:T(128)}, u32[]{:S(2)}) copy-start(s32[2]{0:T(128)} %param.13) | copy-start | bytes 28
  10.8 208.7 %reduce-scatter.2.cloned.1.call-start = ((), (), s32[]{:S(2)}) async-start(), calls=%async_computation.2 | async-start | bytes 557056 | tf_op jit(solution)/shard_map/reduce_scatter | solution.py:67
  11.5 9.9 %collective-permute-start = (bf16[8,1024]{1,0:T(8,128)(2,1)S(1)}, bf16[8,1024]{1,0:T(8,128)(2,1)S(1)}, u32[]{:S(2)}, u32[]{:S(2)}) collective-permute-start(bf16[8,1024]{1,0:T(8,128)(2,1)S(1)} %copy-done), channel_id=1, source_target_pairs={{0,30},{2,0},{4,2},{6,4},{8,6},{10,8},{12,10},{14,12},{16,14},{18,... | collective-permute-start | bytes 49160 | tf_op jit(solution)/shard_map/ppermute | solution.py:39
  21.4 4.0 %collective-permute-start.1 = (bf16[16,1024]{1,0:T(8,128)(2,1)S(1)}, bf16[16,1024]{1,0:T(8,128)(2,1)S(1)}, u32[]{:S(2)}, u32[]{:S(2)}) collective-permute-start(bf16[16,1024]{1,0:T(8,128)(2,1)S(1)} %pad_maximum_fusion.2), channel_id=1, source_target_pairs={{0,28},{2,30},{4,0},{6,2},{8,4},{10,6},{12,8},{14,10},{16,12},{18,... | collective-permute-start | bytes 98312 | tf_op jit(solution)/shard_map/ppermute | solution.py:39
  25.4 4.3 %collective-permute-start.2 = (bf16[32,1024]{1,0:T(8,128)(2,1)S(1)}, bf16[32,1024]{1,0:T(8,128)(2,1)S(1)}, u32[]{:S(2)}, u32[]{:S(2)}) collective-permute-start(bf16[32,1024]{1,0:T(8,128)(2,1)S(1)} %pad_maximum_fusion.1), channel_id=1, source_target_pairs={{0,24},{2,26},{4,28},{6,30},{8,0},{10,2},{12,4},{14,6},{16,8},{18,... | collective-permute-start | bytes 196616 | tf_op jit(solution)/shard_map/ppermute | solution.py:39
  29.7 6.7 %collective-permute-start.3 = (bf16[64,1024]{1,0:T(8,128)(2,1)S(1)}, bf16[64,1024]{1,0:T(8,128)(2,1)S(1)}, u32[]{:S(2)}, u32[]{:S(2)}) collective-permute-start(bf16[64,1024]{1,0:T(8,128)(2,1)S(1)} %pad_maximum_fusion), channel_id=1, source_target_pairs={{0,16},{2,18},{4,20},{6,22},{8,24},{10,26},{12,28},{14,30},{16,0},... | collective-permute-start | bytes 393224 | tf_op jit(solution)/shard_map/ppermute | solution.py:39
  143.7 1.8 copy-start.3
Sparse Core Ops, SparseCore 0:
  10.9 16.3 all-gather.1
  145.6 72.4 reduce-scatter.1
